TPU v7x, 512 devices: a whole 4x8x8 slice. The times are simulated.
512 devices in a mesh: ax: 16 (over y_hi, x), circ: 32 (over y_lo, z, core).
Axes of the slice: x: 4, y: 8 (y_hi: 4, y_lo: 2; y = y_hi * 2 + y_lo), z: 8, core: 2. Of those that a mesh axis runs over, the one named last changes fastest.
Arguments:
- displace: float32 [3, 512, 16384], P(None, 'ax', 'circ'), may hold values from -6 to 6
- load: float32 [3, 512, 16384], P(None, 'ax', 'circ'), may hold values from -6 to 6
- history: float32 [9, 512, 16384], P(None, 'ax', 'circ'), may hold values from -4 to 4
- stiffen: float32 [512, 16384], P('ax', 'circ'), may hold values from 0.2 to 4
- modulus: float32 [9, 9], replicated, may hold values from -2 to 2
- radial_slope: float32 [32, 32], replicated, may hold values from -1 to 1
- radial_basis: float32 [32, 32], replicated, may hold values from -1 to 1
- axial_eig: float32 [512], replicated, may hold values from 0.05 to 4
- cycle_eig: float32 [512], replicated, may hold values from 0.05 to 4
- radial_eig: float32 [32], replicated, may hold values from 0.05 to 4
Outputs:
- precond: float32 [3, 512, 16384], P(None, ('ax', 'circ'))
All inputs are finite; a program needn't handle non-finite values.
Results may differ from a plain program's by a relative error of at most 0.000092.
Values sent between devices are 32-bit elements; how exact they have to be, the bound alone decides.
A program may use at most 64 MiB of HBM per device.

v0:
```python
import math

import jax
import jax.numpy as jnp
import ml_dtypes
import numpy as np
from jax import lax
from jax.experimental import pallas as pl
from jax.experimental.pallas import tpu as pltpu
from jax.sharding import PartitionSpec as P

NA = 512
NC = 512
R = 32
NX = 16
NJ = 32
F32 = jnp.float32
BF16 = jnp.bfloat16
MESH = pl.DeviceIdType.MESH


def cycle_table():
    col = np.arange(NC)[:, None]
    mode = np.arange(NC)[None, :]
    half = NC // 2
    folded = np.where(mode <= half, mode, mode - half)
    shift = np.where(mode <= half, 0.0, 0.5 * np.pi)
    scale = np.where((mode == 0) | (mode == half), math.sqrt(1.0 / NC), math.sqrt(2.0 / NC))
    return np.cos((col * folded % NC) * (2.0 * np.pi / NC) - shift) * scale


def axial_table():
    first = (np.arange(NA) + 1)[:, None]
    mode = (np.arange(NA) + 1)[None, :]
    return np.sin((first * mode % (2 * (NA + 1))) * (np.pi / (NA + 1))) * math.sqrt(2.0 / (NA + 1))


def two_parts(table):
    table = table.astype(np.float32)
    high = table.astype(ml_dtypes.bfloat16)
    low = (table - high.astype(np.float32)).astype(ml_dtypes.bfloat16)
    return np.stack([high, low])


def tables():
    cyc, axi = cycle_table(), axial_table()
    q, cl, j = np.meshgrid(np.arange(4), np.arange(4), np.arange(NJ), indexing="ij")
    cycle_in = cyc[(16 * j + 4 * q + cl).reshape(-1)]
    a4, i, ah = np.meshgrid(np.arange(4), np.arange(NX), np.arange(8), indexing="ij")
    perm = (32 * i + 8 * a4 + ah).reshape(-1)
    c4, cg = np.meshgrid(np.arange(4), np.arange(128), indexing="ij")
    cycle_out = cyc.T[:, (4 * cg + c4).reshape(-1)]
    return np.stack([two_parts(cycle_in), two_parts(axi[perm]), two_parts(axi[:, perm]), two_parts(cycle_out)])


def roll(x, shift):
    return pltpu.roll(x, shift % x.shape[-1], x.ndim - 1)


def parts_of(x):
    high = x.astype(BF16)
    return high, (x - high.astype(F32)).astype(BF16)


def mm(a, b):
    return jnp.dot(a, b, preferred_element_type=F32)


def mm_t(a, b):
    return lax.dot_general(a, b, (((1,), (1,)), ((), ())), preferred_element_type=F32)


def dot3(x, high, low):
    xh, xl = parts_of(x)
    n = x.shape[0]
    both = mm(jnp.concatenate([xh, xl], axis=0), high)
    return both[:n] + (both[n:] + mm(xh, low))


def dot3_t(high, low, x):
    xh, xl = parts_of(x)
    n = high.shape[0]
    both = mm_t(jnp.concatenate([high, low], axis=0), xh)
    return both[:n] + (both[n:] + mm_t(high, xl))


def block_diag(x):
    wide = x + roll(x, 32)
    wide = wide + roll(wide, 64)
    full = jnp.concatenate([wide] * 4, axis=0)
    row = lax.broadcasted_iota(jnp.int32, (128, 128), 0) // 32
    lane = lax.broadcasted_iota(jnp.int32, (128, 128), 1) // 32
    return jnp.where(row == lane, full, 0.0)


def swap_groups(v):
    group = lax.broadcasted_iota(jnp.int32, v[0].shape, 1) // 32
    low_half = group < 2
    a0 = jnp.where(low_half, v[0], roll(v[2], 64))
    a2 = jnp.where(low_half, roll(v[0], 64), v[2])
    a1 = jnp.where(low_half, v[1], roll(v[3], 64))
    a3 = jnp.where(low_half, roll(v[1], 64), v[3])
    even = (group % 2) == 0
    u0 = jnp.where(even, a0, roll(a1, 32))
    u1 = jnp.where(even, roll(a0, -32), a1)
    u2 = jnp.where(even, a2, roll(a3, 32))
    u3 = jnp.where(even, roll(a2, -32), a3)
    return [u0, u1, u2, u3]


def tiles(x):
    return [x[:, 128 * t : 128 * (t + 1)] for t in range(x.shape[1] // 128)]


def rows(x, n):
    return [x[n * t : n * (t + 1)] for t in range(x.shape[0] // n)]


def smooth_a(up, mid, down):
    return (up + 4.0 * mid + down) * (1.0 / 6.0)


def slope_a(up, down):
    return (down - up) * 0.5


def smooth_c(x):
    return (roll(x, 32) + 4.0 * x + roll(x, -32)) * (1.0 / 6.0)


def slope_c(x):
    return (roll(x, -32) - roll(x, 32)) * 0.5


def gradients(windows, slope_t):
    first, second, plain = [], [], []
    for up, mid, down in windows:
        first.append(smooth_c(slope_a(up, down)))
        smooth = smooth_a(up, mid, down)
        second.append(slope_c(smooth))
        plain.append(smooth_c(smooth))
    stacked = jnp.concatenate([t for x in plain for t in tiles(x)], axis=0)
    mixed = rows(dot3(stacked, *slope_t), 40)
    third = [jnp.concatenate(mixed[6 * p : 6 * p + 6], axis=1) for p in range(3)]
    return first + second + third


def pulled(load, stress, p):
    up, _, down = stress(p)
    part = smooth_c(slope_a(up, down))
    part = part + slope_c(smooth_a(*stress(3 + p)))
    third = smooth_c(smooth_a(*stress(6 + p)))
    near = load + part[:, 128:640]
    return jnp.concatenate(tiles(near), axis=0), jnp.concatenate(tiles(third[:, 128:640]), axis=0)


def cycle_forward(parts, high, low):
    lhs = []
    for x in parts:
        lhs.append(jnp.concatenate(rows(x.T, 32), axis=1))
    y = dot3(jnp.concatenate(lhs, axis=0), high, low)
    out = []
    for p in range(3):
        block = tiles(y[32 * p : 32 * p + 32])
        out.append([swap_groups(rows(t, 8)) for t in block])
    return out


def axial_solve(parts, denom, forward, inverse):
    lhs = jnp.concatenate([jnp.concatenate(rows(x.T, 32), axis=1) for x in parts], axis=0)
    modes = dot3(lhs, *forward)
    modes = modes / jnp.concatenate([denom] * 3, axis=0)
    y = dot3(modes, *inverse)
    return [jnp.concatenate(tiles(x), axis=0).T for x in rows(y, 32)]


def cycle_inverse(parts, high, low):
    lhs = []
    for p in range(3):
        cols = [jnp.concatenate(swap_groups(parts[p][it]), axis=0) for it in range(4)]
        lhs.append(jnp.concatenate(cols, axis=1))
    return dot3(jnp.concatenate(lhs, axis=0), high, low)


def radial_inverse(parts, high, low):
    return dot3(jnp.concatenate([x.T for x in parts], axis=0), high, low)


def kernel(
    displace, load, history, stiffen, table, slope_ref, basis_ref, axial_ref, cycle_ref, modulus, radial,
    out,
    dext, hext, sext, load_v, table_v, pad_v, rsend, rtop, rbot, corner, stress_v,
    s1, r1, s2, r2, s3, r3, s4, r4, out_v,
    in_sem, table_sem, halo_send, halo_recv, a2a_send, a2a_recv, out_sem,
):
    i = lax.axis_index("ax")
    j = lax.axis_index("circ")
    up_i, down_i = lax.rem(i + NX - 1, NX), lax.rem(i + 1, NX)
    left_j, right_j = lax.rem(j + NJ - 1, NJ), lax.rem(j + 1, NJ)

    own = [
        pltpu.make_async_copy(displace, dext.at[:, 8:40, 128:640], in_sem.at[0]),
        pltpu.make_async_copy(history, hext.at[:, 8:40, 128:640], in_sem.at[1]),
        pltpu.make_async_copy(stiffen, sext.at[8:40, 128:640], in_sem.at[2]),
        pltpu.make_async_copy(load, load_v, in_sem.at[3]),
    ]
    for copy in own:
        copy.start()
    table_copies = [pltpu.make_async_copy(table.at[k], table_v.at[k], table_sem.at[k]) for k in range(4)]

    barrier = pltpu.get_barrier_semaphore()

    def greet_circ(s, carry):
        pl.semaphore_signal(barrier, inc=1, device_id=(i, lax.rem(j + s, NJ)), device_id_type=MESH)
        return carry

    def greet_ax(s, carry):
        pl.semaphore_signal(barrier, inc=1, device_id=(lax.rem(i + s, NX), j), device_id_type=MESH)
        return carry

    for di in (up_i, down_i):
        for dj in (left_j, right_j):
            pl.semaphore_signal(barrier, inc=1, device_id=(di, dj), device_id_type=MESH)
    lax.fori_loop(1, NX, greet_ax, 0)
    lax.fori_loop(1, NJ, greet_circ, 0)
    for copy in table_copies:
        copy.start()

    for copy in own[:3]:
        copy.wait()
    for side, (d0, h0) in enumerate(((8, 8), (38, 39))):
        for p in range(3):
            rsend[side, 2 * p : 2 * p + 2, :] = dext[p, d0 : d0 + 2, 128:640]
        for n in range(9):
            rsend[side, 6 + n : 7 + n, :] = hext[n, h0 : h0 + 1, 128:640]
        rsend[side, 15:16, :] = sext[h0 : h0 + 1, 128:640]

    pl.semaphore_wait(barrier, NJ - 1 + NX - 1 + 4)

    copies = []

    def send(src, dst, device):
        k = len(copies)
        copy = pltpu.make_async_remote_copy(
            src_ref=src, dst_ref=dst, send_sem=halo_send.at[k], recv_sem=halo_recv.at[k],
            device_id=device, device_id_type=MESH,
        )
        copy.start()
        copies.append(copy)

    send(rsend.at[1], rtop, (down_i, j))
    send(rsend.at[0], rbot, (up_i, j))
    send(displace.at[:, :, 384:512], dext.at[:, 8:40, 0:128], (i, right_j))
    send(displace.at[:, :, 0:128], dext.at[:, 8:40, 640:768], (i, left_j))
    send(history.at[:, :, 384:512], hext.at[:, 8:40, 0:128], (i, right_j))
    send(history.at[:, :, 0:128], hext.at[:, 8:40, 640:768], (i, left_j))
    send(stiffen.at[:, 384:512], sext.at[8:40, 0:128], (i, right_j))
    send(stiffen.at[:, 0:128], sext.at[8:40, 640:768], (i, left_j))
    send(rsend.at[1, :, 384:512], corner.at[0, 0], (down_i, right_j))
    send(rsend.at[1, :, 0:128], corner.at[0, 1], (down_i, left_j))
    send(rsend.at[0, :, 384:512], corner.at[1, 0], (up_i, right_j))
    send(rsend.at[0, :, 0:128], corner.at[1, 1], (up_i, left_j))

    pad_v[...] = jnp.zeros_like(pad_v)
    pad_v[0, :, 0:32] = slope_ref[...]
    pad_v[1, :, 0:32] = basis_ref[...]
    slope = block_diag(pad_v[0])
    slope_t = slope.T
    basis_t = block_diag(pad_v[1]).T
    slope, slope_t, basis_t = parts_of(slope), parts_of(slope_t), parts_of(basis_t)
    lane = lax.broadcasted_iota(jnp.int32, (32, NC), 1)
    row = lax.broadcasted_iota(jnp.int32, (32, NC), 0)
    picked = jnp.where(lane == row + 32 * i, jnp.broadcast_to(cycle_ref[...], (32, NC)), 0.0)
    denom = axial_ref[...] + jnp.sum(picked, axis=1, keepdims=True) + radial[j]

    for copy in copies:
        copy.wait_recv()
    not_first, not_last = i > 0, i < NX - 1
    for side, (ref, d0, h0, there) in enumerate(((rtop, 6, 7, not_first), (rbot, 40, 40, not_last))):
        whole = jnp.concatenate([corner[side, 0], ref[...], corner[side, 1]], axis=1)
        whole = jnp.where(there, whole, 0.0)
        for p in range(3):
            dext[p, d0 : d0 + 2, :] = whole[2 * p : 2 * p + 2]
        for n in range(9):
            hext[n, h0 : h0 + 1, :] = whole[6 + n : 7 + n]
        sext[h0 : h0 + 1, :] = whole[15:16]

    windows = [(dext[p, 6:46, :], dext[p, 7:47, :], dext[p, 8:48, :]) for p in range(3)]
    grads = gradients(windows, slope_t)
    inside = lax.broadcasted_iota(jnp.int32, (40, 128), 0)
    keep = ((inside > 0) | not_first) & ((inside < 33) | not_last)
    for t in range(6):
        cols = slice(128 * t, 128 * (t + 1))
        piece = [g[:, cols] for g in grads]
        factor = 1.0 + sext[7:47, cols]
        for m in range(9):
            total = modulus[m, 0] * piece[0]
            for n in range(1, 9):
                total = total + modulus[m, n] * piece[n]
            stress_v[m, :, cols] = jnp.where(keep, factor * total + hext[m, 7:47, cols], 0.0)

    def stress(m):
        return stress_v[m, 0:32, :], stress_v[m, 1:33, :], stress_v[m, 2:34, :]

    own[3].wait()
    near, far = [], []
    for p in range(3):
        a, b = pulled(load_v[p], stress, p)
        near.append(a)
        far.append(b)
    resid = jnp.concatenate(near, axis=0) - dot3(jnp.concatenate(far, axis=0), *slope)

    for p in range(3):
        mixed = dot3_t(*basis_t, resid[128 * p : 128 * (p + 1)])
        for cl in range(4):
            s1[:, 4 * p + cl, :] = mixed[32 * cl : 32 * cl + 32]

    def exchange(k, src, dst, count, me, device):
        pltpu.make_async_copy(src.at[me], dst.at[me], a2a_recv.at[k]).start()

        def push(s, carry):
            d = lax.rem(me + s, count)
            pltpu.make_async_remote_copy(
                src_ref=src.at[d], dst_ref=dst.at[me], send_sem=a2a_send.at[k], recv_sem=a2a_recv.at[k],
                device_id=device(d), device_id_type=MESH,
            ).start()
            return carry

        lax.fori_loop(1, count, push, 0)
        pltpu.make_async_copy(dst, dst, a2a_recv.at[k]).wait()

    on_circ = lambda d: (i, d)
    on_ax = lambda d: (d, j)

    exchange(0, s1, r1, NJ, j, on_circ)
    table_copies[0].wait()
    lines = [jnp.concatenate([r1[:, 4 * p + cl, :] for cl in range(4)], axis=0) for p in range(3)]
    blocks = cycle_forward(lines, table_v[0, 0], table_v[0, 1])
    for p in range(3):
        for it in range(4):
            for i4 in range(4):
                s2[4 * it + i4, p] = blocks[p][it][i4]

    exchange(1, s2, r2, NX, i, on_ax)
    table_copies[1].wait()
    table_copies[2].wait()
    lines = [r2[:, p].reshape(128, 128) for p in range(3)]
    solved = axial_solve(lines, denom, (table_v[1, 0], table_v[1, 1]), (table_v[2, 0], table_v[2, 1]))
    for p in range(3):
        s3[:, p] = solved[p].reshape(NX, 8, 128)

    exchange(2, s3, r3, NX, i, on_ax)
    table_copies[3].wait()
    blocks = [[[r3[4 * it + i4, p] for i4 in range(4)] for it in range(4)] for p in range(3)]
    y = cycle_inverse(blocks, table_v[3, 0], table_v[3, 1])
    for p in range(3):
        for c4 in range(4):
            s4[:, 4 * p + c4, :] = y[32 * p : 32 * p + 32, 128 * c4 : 128 * (c4 + 1)]

    exchange(3, s4, r4, NJ, j, on_circ)
    lines = [jnp.concatenate([r4[:, 4 * p + c4, :] for c4 in range(4)], axis=0) for p in range(3)]
    out_v[...] = radial_inverse(lines, *basis_t)
    last = pltpu.make_async_copy(out_v, out, out_sem.at[0])
    last.start()

    for copy in copies:
        copy.wait_send()
    for k, (ref, count) in enumerate(((s1, NJ), (s2, NX), (s3, NX), (s4, NJ))):
        sent = ref.at[pl.ds(0, count - 1)]
        pltpu.make_async_copy(sent, sent, a2a_send.at[k]).wait()
    last.wait()


def solution(mesh):
    table = tables()

    def body(displace, load, history, stiffen, modulus, slope, basis, axial, cycle, radial):
        hbm = pl.BlockSpec(memory_space=pl.ANY)
        vmem = pl.BlockSpec(memory_space=pltpu.VMEM)
        smem = pl.BlockSpec(memory_space=pltpu.SMEM)
        dma = pltpu.SemaphoreType.DMA
        out = pl.pallas_call(
            kernel,
            out_shape=jax.ShapeDtypeStruct((384, 128), F32),
            in_specs=[hbm] * 5 + [vmem] * 4 + [smem] * 2,
            out_specs=hbm,
            scratch_shapes=[
                pltpu.VMEM((3, 48, 768), F32),
                pltpu.VMEM((9, 48, 768), F32),
                pltpu.VMEM((48, 768), F32),
                pltpu.VMEM((3, 32, 512), F32),
                pltpu.VMEM((4, 2, 512, 512), BF16),
                pltpu.VMEM((2, 32, 128), F32),
                pltpu.VMEM((2, 16, 512), F32),
                pltpu.VMEM((16, 512), F32),
                pltpu.VMEM((16, 512), F32),
                pltpu.VMEM((2, 2, 16, 128), F32),
                pltpu.VMEM((9, 40, 768), F32),
                pltpu.VMEM((NJ, 12, 128), F32),
                pltpu.VMEM((NJ, 12, 128), F32),
                pltpu.VMEM((NX, 3, 8, 128), F32),
                pltpu.VMEM((NX, 3, 8, 128), F32),
                pltpu.VMEM((NX, 3, 8, 128), F32),
                pltpu.VMEM((NX, 3, 8, 128), F32),
                pltpu.VMEM((NJ, 12, 128), F32),
                pltpu.VMEM((NJ, 12, 128), F32),
                pltpu.VMEM((384, 128), F32),
                dma((4,)),
                dma((4,)),
                dma((12,)),
                dma((12,)),
                dma((4,)),
                dma((4,)),
                dma((1,)),
            ],
            compiler_params=pltpu.CompilerParams(
                collective_id=0, has_side_effects=True, vmem_limit_bytes=48 * 1024 * 1024
            ),
        )(
            displace, load, history, stiffen, jnp.asarray(table), slope, basis,
            axial.reshape(1, NA), cycle.reshape(1, NC), modulus, radial,
        )
        return out.reshape(3, 1, NC * R)

    return jax.shard_map(
        body,
        mesh=mesh,
        in_specs=(
            P(None, "ax", "circ"),
            P(None, "ax", "circ"),
            P(None, "ax", "circ"),
            P("ax", "circ"),
            P(),
            P(),
            P(),
            P(),
            P(),
            P(),
        ),
        out_specs=P(None, ("ax", "circ"), None),
        check_vma=False,
    )
```

profile of v0, /device:TPU:1, one launch (start us, length us, event | category | flops | bytes accessed | tf_op | source)
XLA Modules:
  0.0 70.9 jit_solution(8244464673047839637)
XLA Ops:
  0.0 0.0 copy-start
  0.0 2.2 %copy-done = bf16[4,2,512,512]{3,2,1,0:T(8,128)(2,1)S(1)} copy-done((bf16[4,2,512,512]{3,2,1,0:T(8,128)(2,1)S(1)}, bf16[4,2,512,512]{3,2,1,0:T(8,128)(2,1)}, u32[]{:S(2)}) %copy-start) | copy-done | bytes 4194328
  2.2 0.0 copy-start.1
  2.2 1.1 %copy-done.1 = f32[9,32,512]{2,1,0:T(8,128)S(1)} copy-done((f32[9,32,512]{2,1,0:T(8,128)S(1)}, f32[9,32,512]{2,1,0:T(8,128)}, u32[]{:S(2)}) %copy-start.1) | copy-done | bytes 589848
  3.3 0.0 copy-start.2
  3.3 0.9 %copy-done.2 = f32[3,32,512]{2,1,0:T(8,128)S(1)} copy-done((f32[3,32,512]{2,1,0:T(8,128)S(1)}, f32[3,32,512]{2,1,0:T(8,128)}, u32[]{:S(2)}) %copy-start.2) | copy-done | bytes 196632
  4.2 0.0 copy-start.3
  4.2 0.9 %copy-done.3 = f32[3,32,512]{2,1,0:T(8,128)S(1)} copy-done((f32[3,32,512]{2,1,0:T(8,128)S(1)}, f32[3,32,512]{2,1,0:T(8,128)}, u32[]{:S(2)}) %copy-start.3) | copy-done | bytes 196632
  5.1 0.0 copy-start.4
  5.1 0.8 %copy-done.4 = f32[32,512]{1,0:T(8,128)S(1)} copy-done((f32[32,512]{1,0:T(8,128)S(1)}, f32[32,512]{1,0:T(8,128)}, u32[]{:S(2)}) %copy-start.4) | copy-done | bytes 65560
  5.9 0.0 copy-start.5
  6.0 0.7 %copy-done.5 = f32[32,32]{1,0:T(8,128)S(1)} copy-done((f32[32,32]{1,0:T(8,128)S(1)}, f32[32,32]{1,0:T(8,128)}, u32[]{:S(2)}) %copy-start.5) | copy-done | bytes 4120
  6.7 0.0 copy-start.6
  6.7 0.7 %copy-done.6 = f32[32,32]{1,0:T(8,128)S(1)} copy-done((f32[32,32]{1,0:T(8,128)S(1)}, f32[32,32]{1,0:T(8,128)}, u32[]{:S(2)}) %copy-start.6) | copy-done | bytes 4120
  7.4 0.0 copy-start.7
  7.4 0.7 copy-done.7
  8.1 0.0 copy-start.8
  8.1 0.7 copy-done.8
  8.8 0.0 copy-start.9
  8.8 0.7 copy-done.9
  9.4 0.0 copy-start.10
  9.4 0.7 copy-done.10
  10.1 60.1 %shard_map.109 = f32[384,128]{1,0:T(8,128)S(1)} custom-call(f32[3,32,512]{2,1,0:T(8,128)S(1)} %copy-done.2, f32[3,32,512]{2,1,0:T(8,128)S(1)} %copy-done.3, f32[9,32,512]{2,1,0:T(8,128)S(1)} %copy-done.1, f32[32,512]{1,0:T(8,128)S(1)} %copy-done.4, bf16[4,2,512,512]{3,2,1,0:T(8,128)(2,1)S(1)} %copy-done, f32[32,32]{1,0:T(8,128)S(1)} %copy-done.5, ...), custom_call_target="tpu_custom_call" | custom-call | tf_op jit(solution)/shard_map/pallas_call | solution.py:382
  70.2 0.7 copy.15
Async XLA Ops:
  0.0 2.2 %copy-start = (bf16[4,2,512,512]{3,2,1,0:T(8,128)(2,1)S(1)}, bf16[4,2,512,512]{3,2,1,0:T(8,128)(2,1)}, u32[]{:S(2)}) copy-start(bf16[4,2,512,512]{3,2,1,0:T(8,128)(2,1)} %constant.2.clone.table) | copy-start | bytes 12582916
  2.2 1.1 %copy-start.1 = (f32[9,32,512]{2,1,0:T(8,128)S(1)}, f32[9,32,512]{2,1,0:T(8,128)}, u32[]{:S(2)}) copy-start(f32[9,32,512]{2,1,0:T(8,128)} %history.1) | copy-start | bytes 1769476
  3.3 0.9 %copy-start.2 = (f32[3,32,512]{2,1,0:T(8,128)S(1)}, f32[3,32,512]{2,1,0:T(8,128)}, u32[]{:S(2)}) copy-start(f32[3,32,512]{2,1,0:T(8,128)} %displace.1) | copy-start | bytes 589828
  4.2 0.9 %copy-start.3 = (f32[3,32,512]{2,1,0:T(8,128)S(1)}, f32[3,32,512]{2,1,0:T(8,128)}, u32[]{:S(2)}) copy-start(f32[3,32,512]{2,1,0:T(8,128)} %load.1) | copy-start | bytes 589828
  5.1 0.8 %copy-start.4 = (f32[32,512]{1,0:T(8,128)S(1)}, f32[32,512]{1,0:T(8,128)}, u32[]{:S(2)}) copy-start(f32[32,512]{1,0:T(8,128)} %stiffen.1) | copy-start | bytes 196612
  5.9 0.7 %copy-start.5 = (f32[32,32]{1,0:T(8,128)S(1)}, f32[32,32]{1,0:T(8,128)}, u32[]{:S(2)}) copy-start(f32[32,32]{1,0:T(8,128)} %slope_ref.1) | copy-start | bytes 12292
  6.7 0.7 %copy-start.6 = (f32[32,32]{1,0:T(8,128)S(1)}, f32[32,32]{1,0:T(8,128)}, u32[]{:S(2)}) copy-start(f32[32,32]{1,0:T(8,128)} %basis_ref.1) | copy-start | bytes 12292
  7.4 0.7 copy-start.7
  8.1 0.7 copy-start.8
  8.8 0.7 copy-start.9
  9.4 0.7 copy-start.10
where the time goes:
time: 71.4 us; the launch traced here: 70.9 us
  Pallas kernels  60.1 us (84%)
  local copies, waits for them, and re-layouts  10.8 us (15%)
    pallas_call x1, Pallas kernels, body(): pl.pallas_call(kernel, out_shape=jax.ShapeDtypeStruct((384, 128), F32), i...  60.1 us
    unnamed x23, local copies, waits for them, and re-layouts  10.8 us

commit v1 on v0

--- a/solution.py
+++ b/solution.py
@@ -187,11 +187,12 @@
 
 
 def kernel(
-    displace, load, history, stiffen, table, slope_ref, basis_ref, axial_ref, cycle_ref, modulus, radial,
-    out,
+    displace, load, history, stiffen, table, slope_hbm, basis_hbm, axial_hbm, cycle_hbm, modulus_hbm, radial_hbm,
+    out_v,
+    slope_ref, basis_ref, axial_ref, cycle_ref, modulus, radial,
     dext, hext, sext, load_v, table_v, pad_v, rsend, rtop, rbot, corner, stress_v,
-    s1, r1, s2, r2, s3, r3, s4, r4, out_v,
-    in_sem, table_sem, halo_send, halo_recv, a2a_send, a2a_recv, out_sem,
+    s1, r1, s2, r2, s3, r3, s4, r4,
+    in_sem, table_sem, halo_send, halo_recv, a2a_send, a2a_recv,
 ):
     i = lax.axis_index("ax")
     j = lax.axis_index("circ")
@@ -202,7 +203,13 @@
         pltpu.make_async_copy(displace, dext.at[:, 8:40, 128:640], in_sem.at[0]),
         pltpu.make_async_copy(history, hext.at[:, 8:40, 128:640], in_sem.at[1]),
         pltpu.make_async_copy(stiffen, sext.at[8:40, 128:640], in_sem.at[2]),
-        pltpu.make_async_copy(load, load_v, in_sem.at[3]),
+        pltpu.make_async_copy(slope_hbm, slope_ref, in_sem.at[3]),
+        pltpu.make_async_copy(basis_hbm, basis_ref, in_sem.at[4]),
+        pltpu.make_async_copy(axial_hbm, axial_ref, in_sem.at[5]),
+        pltpu.make_async_copy(cycle_hbm, cycle_ref, in_sem.at[6]),
+        pltpu.make_async_copy(modulus_hbm, modulus, in_sem.at[7]),
+        pltpu.make_async_copy(radial_hbm, radial, in_sem.at[8]),
+        pltpu.make_async_copy(load, load_v, in_sem.at[9]),
     ]
     for copy in own:
         copy.start()
@@ -261,6 +268,8 @@
     send(rsend.at[0, :, 384:512], corner.at[1, 0], (up_i, right_j))
     send(rsend.at[0, :, 0:128], corner.at[1, 1], (up_i, left_j))
 
+    for copy in own[3:]:
+        copy.wait()
     pad_v[...] = jnp.zeros_like(pad_v)
     pad_v[0, :, 0:32] = slope_ref[...]
     pad_v[1, :, 0:32] = basis_ref[...]
@@ -302,7 +311,6 @@
     def stress(m):
         return stress_v[m, 0:32, :], stress_v[m, 1:33, :], stress_v[m, 2:34, :]
 
-    own[3].wait()
     near, far = [], []
     for p in range(3):
         a, b = pulled(load_v[p], stress, p)
@@ -360,31 +368,32 @@
     exchange(3, s4, r4, NJ, j, on_circ)
     lines = [jnp.concatenate([r4[:, 4 * p + c4, :] for c4 in range(4)], axis=0) for p in range(3)]
     out_v[...] = radial_inverse(lines, *basis_t)
-    last = pltpu.make_async_copy(out_v, out, out_sem.at[0])
-    last.start()
 
     for copy in copies:
         copy.wait_send()
     for k, (ref, count) in enumerate(((s1, NJ), (s2, NX), (s3, NX), (s4, NJ))):
         sent = ref.at[pl.ds(0, count - 1)]
         pltpu.make_async_copy(sent, sent, a2a_send.at[k]).wait()
-    last.wait()
 
 
 def solution(mesh):
     table = tables()
 
     def body(displace, load, history, stiffen, modulus, slope, basis, axial, cycle, radial):
-        hbm = pl.BlockSpec(memory_space=pl.ANY)
-        vmem = pl.BlockSpec(memory_space=pltpu.VMEM)
-        smem = pl.BlockSpec(memory_space=pltpu.SMEM)
+        hbm = pl.BlockSpec(memory_space=pltpu.HBM)
         dma = pltpu.SemaphoreType.DMA
         out = pl.pallas_call(
             kernel,
             out_shape=jax.ShapeDtypeStruct((384, 128), F32),
-            in_specs=[hbm] * 5 + [vmem] * 4 + [smem] * 2,
-            out_specs=hbm,
+            in_specs=[hbm] * 11,
+            out_specs=pl.BlockSpec(memory_space=pltpu.VMEM),
             scratch_shapes=[
+                pltpu.VMEM((R, R), F32),
+                pltpu.VMEM((R, R), F32),
+                pltpu.VMEM((1, NA), F32),
+                pltpu.VMEM((1, NC), F32),
+                pltpu.SMEM((9, 9), F32),
+                pltpu.SMEM((R,), F32),
                 pltpu.VMEM((3, 48, 768), F32),
                 pltpu.VMEM((9, 48, 768), F32),
                 pltpu.VMEM((48, 768), F32),
@@ -404,17 +413,15 @@
                 pltpu.VMEM((NX, 3, 8, 128), F32),
                 pltpu.VMEM((NJ, 12, 128), F32),
                 pltpu.VMEM((NJ, 12, 128), F32),
-                pltpu.VMEM((384, 128), F32),
-                dma((4,)),
+                dma((10,)),
                 dma((4,)),
                 dma((12,)),
                 dma((12,)),
                 dma((4,)),
                 dma((4,)),
-                dma((1,)),
             ],
             compiler_params=pltpu.CompilerParams(
-                collective_id=0, has_side_effects=True, vmem_limit_bytes=48 * 1024 * 1024
+                collective_id=0, has_side_effects=True, vmem_limit_bytes=60 * 1024 * 1024
             ),
         )(
             displace, load, history, stiffen, jnp.asarray(table), slope, basis,

time: 71.4 us -> 61.1 us (0.86)
  local copies, waits for them, and re-layouts: 10.8 us -> 1.62 us
    unnamed x23 -> x1, local copies, waits for them, and re-layouts: 10.8 us -> 1.62 us
    pallas_call x1, Pallas kernels: 60.1 us -> 59.4 us  [body(): pl.pallas_call(kernel, out_shape=jax.ShapeDtypeStruct((384, 128), F32), i...]
where the time goes in v1:
time: 61.1 us; the launch traced here: 61 us
  Pallas kernels  59.4 us (97%)
  local copies, waits for them, and re-layouts  1.62 us (3%)
    pallas_call x1, Pallas kernels, body(): pl.pallas_call(kernel, out_shape=jax.ShapeDtypeStruct((384, 128), F32), i...  59.4 us
    unnamed x1, local copies, waits for them, and re-layouts  1.62 us

profile of v1, /device:TPU:1, one launch (start us, length us, event | category | flops | bytes accessed | tf_op | source)
XLA Modules:
  0.0 61.0 jit_solution(8092791605936325664)
XLA Ops:
  0.0 59.4 %shard_map.109 = f32[384,128]{1,0:T(8,128)} custom-call(f32[3,32,512]{2,1,0:T(8,128)} %displace.1, f32[3,32,512]{2,1,0:T(8,128)} %load.1, f32[9,32,512]{2,1,0:T(8,128)} %history.1, f32[32,512]{1,0:T(8,128)} %stiffen.1, bf16[4,2,512,512]{3,2,1,0:T(8,128)(2,1)} %constant.2.clone.table, f32[32,32]{1,0:T(8,128)} %slope_hbm.1, f32[32,32]{1,0:T(8,128)} %basis_hbm.1, ...), custom_call_target="tpu_custom_call" | custom-call | tf_op jit(solution)/shard_map/pallas_call | solution.py:385
  59.4 1.6 %copy.15 = f32[3,1,16384]{2,1,0:T(1,128)} copy(f32[3,1,16384]{2,1,0:T(1,128)} %bitcast.3) | data formatting | bytes 393216

commit v2 on v1

--- a/solution.py
+++ b/solution.py
@@ -154,43 +154,56 @@
     return jnp.concatenate(tiles(near), axis=0), jnp.concatenate(tiles(third[:, 128:640]), axis=0)
 
 
-def cycle_forward(parts, high, low):
-    lhs = []
-    for x in parts:
-        lhs.append(jnp.concatenate(rows(x.T, 32), axis=1))
-    y = dot3(jnp.concatenate(lhs, axis=0), high, low)
-    out = []
-    for p in range(3):
-        block = tiles(y[32 * p : 32 * p + 32])
-        out.append([swap_groups(rows(t, 8)) for t in block])
+def cycle_forward(x, high, low):
+    y = dot3(jnp.concatenate(rows(x.T, 32), axis=1), high, low)
+    return [swap_groups(rows(t, 8)) for t in tiles(y)]
+
+
+def axial_solve(x, denom, forward, inverse):
+    modes = dot3(jnp.concatenate(rows(x.T, 32), axis=1), *forward)
+    y = dot3(modes / denom, *inverse)
+    return jnp.concatenate(tiles(y), axis=0).T
+
+
+def cycle_inverse(blocks, high, low):
+    cols = [jnp.concatenate(swap_groups(four), axis=0) for four in blocks]
+    return dot3(jnp.concatenate(cols, axis=1), high, low)
+
+
+def pack_columns(fields, last):
+    lane = lax.broadcasted_iota(jnp.int32, (32, 128), 1)
+
+    def move(x, width, at):
+        start = 128 - width if last else 0
+        return roll(x, at - start) if at != start else x
+
+    two = jnp.where(lane < 64, move(fields[0], 64, 0), move(fields[1], 64, 64))
+    mixed = jnp.where(lane < 96, move(fields[3], 32, 64), move(fields[4], 32, 96))
+    out = [two, jnp.where(lane < 64, move(fields[2], 64, 0), mixed)]
+    for first in (5, 9):
+        low = jnp.where(lane < 32, move(fields[first], 32, 0), move(fields[first + 1], 32, 32))
+        high = jnp.where(lane < 96, move(fields[first + 2], 32, 64), move(fields[first + 3], 32, 96))
+        out.append(jnp.where(lane < 64, low, high))
     return out
 
 
-def axial_solve(parts, denom, forward, inverse):
-    lhs = jnp.concatenate([jnp.concatenate(rows(x.T, 32), axis=1) for x in parts], axis=0)
-    modes = dot3(lhs, *forward)
-    modes = modes / jnp.concatenate([denom] * 3, axis=0)
-    y = dot3(modes, *inverse)
-    return [jnp.concatenate(tiles(x), axis=0).T for x in rows(y, 32)]
-
-
-def cycle_inverse(parts, high, low):
-    lhs = []
-    for p in range(3):
-        cols = [jnp.concatenate(swap_groups(parts[p][it]), axis=0) for it in range(4)]
-        lhs.append(jnp.concatenate(cols, axis=1))
-    return dot3(jnp.concatenate(lhs, axis=0), high, low)
-
-
-def radial_inverse(parts, high, low):
-    return dot3(jnp.concatenate([x.T for x in parts], axis=0), high, low)
+def unpack_columns(packed, last):
+    def move(x, width, at):
+        end = 128 - width if last else 0
+        return roll(x, end - at) if at != end else x
+
+    out = [move(packed[0], 64, 0), move(packed[0], 64, 64), move(packed[1], 64, 0)]
+    out += [move(packed[1], 32, 64), move(packed[1], 32, 96)]
+    for t in (2, 3):
+        out += [move(packed[t], 32, 32 * g) for g in range(4)]
+    return out
 
 
 def kernel(
     displace, load, history, stiffen, table, slope_hbm, basis_hbm, axial_hbm, cycle_hbm, modulus_hbm, radial_hbm,
     out_v,
     slope_ref, basis_ref, axial_ref, cycle_ref, modulus, radial,
-    dext, hext, sext, load_v, table_v, pad_v, rsend, rtop, rbot, corner, stress_v,
+    dext, hext, sext, load_v, table_v, pad_v, rsend, csend, rtop, rbot, cleft, cright, corner, stress_v,
     s1, r1, s2, r2, s3, r3, s4, r4,
     in_sem, table_sem, halo_send, halo_recv, a2a_send, a2a_recv,
 ):
@@ -242,6 +255,11 @@
             rsend[side, 6 + n : 7 + n, :] = hext[n, h0 : h0 + 1, 128:640]
         rsend[side, 15:16, :] = sext[h0 : h0 + 1, 128:640]
 
+    for side, cols in enumerate((slice(128, 256), slice(512, 640))):
+        edge = [dext[p, 8:40, cols] for p in range(3)] + [hext[n, 8:40, cols] for n in range(9)] + [sext[8:40, cols]]
+        for t, value in enumerate(pack_columns(edge, side == 1)):
+            csend[side, t] = value
+
     pl.semaphore_wait(barrier, NJ - 1 + NX - 1 + 4)
 
     copies = []
@@ -257,12 +275,8 @@
 
     send(rsend.at[1], rtop, (down_i, j))
     send(rsend.at[0], rbot, (up_i, j))
-    send(displace.at[:, :, 384:512], dext.at[:, 8:40, 0:128], (i, right_j))
-    send(displace.at[:, :, 0:128], dext.at[:, 8:40, 640:768], (i, left_j))
-    send(history.at[:, :, 384:512], hext.at[:, 8:40, 0:128], (i, right_j))
-    send(history.at[:, :, 0:128], hext.at[:, 8:40, 640:768], (i, left_j))
-    send(stiffen.at[:, 384:512], sext.at[8:40, 0:128], (i, right_j))
-    send(stiffen.at[:, 0:128], sext.at[8:40, 640:768], (i, left_j))
+    send(csend.at[1], cleft, (i, right_j))
+    send(csend.at[0], cright, (i, left_j))
     send(rsend.at[1, :, 384:512], corner.at[0, 0], (down_i, right_j))
     send(rsend.at[1, :, 0:128], corner.at[0, 1], (down_i, left_j))
     send(rsend.at[0, :, 384:512], corner.at[1, 0], (up_i, right_j))
@@ -285,6 +299,13 @@
     for copy in copies:
         copy.wait_recv()
     not_first, not_last = i > 0, i < NX - 1
+    for ref, cols, left in ((cleft, slice(0, 128), True), (cright, slice(640, 768), False)):
+        fields = unpack_columns([ref[t] for t in range(4)], left)
+        for p in range(3):
+            dext[p, 8:40, cols] = fields[p]
+        for n in range(9):
+            hext[n, 8:40, cols] = fields[3 + n]
+        sext[8:40, cols] = fields[12]
     for side, (ref, d0, h0, there) in enumerate(((rtop, 6, 7, not_first), (rbot, 40, 40, not_last))):
         whole = jnp.concatenate([corner[side, 0], ref[...], corner[side, 1]], axis=1)
         whole = jnp.where(there, whole, 0.0)
@@ -311,68 +332,68 @@
     def stress(m):
         return stress_v[m, 0:32, :], stress_v[m, 1:33, :], stress_v[m, 2:34, :]
 
-    near, far = [], []
-    for p in range(3):
-        a, b = pulled(load_v[p], stress, p)
-        near.append(a)
-        far.append(b)
-    resid = jnp.concatenate(near, axis=0) - dot3(jnp.concatenate(far, axis=0), *slope)
-
-    for p in range(3):
-        mixed = dot3_t(*basis_t, resid[128 * p : 128 * (p + 1)])
-        for cl in range(4):
-            s1[:, 4 * p + cl, :] = mixed[32 * cl : 32 * cl + 32]
-
-    def exchange(k, src, dst, count, me, device):
-        pltpu.make_async_copy(src.at[me], dst.at[me], a2a_recv.at[k]).start()
+    def start(k, p, src, dst, count, me, device):
+        pltpu.make_async_copy(src.at[p, me], dst.at[p, me], a2a_recv.at[k, p]).start()
 
         def push(s, carry):
             d = lax.rem(me + s, count)
             pltpu.make_async_remote_copy(
-                src_ref=src.at[d], dst_ref=dst.at[me], send_sem=a2a_send.at[k], recv_sem=a2a_recv.at[k],
+                src_ref=src.at[p, d], dst_ref=dst.at[p, me], send_sem=a2a_send.at[k], recv_sem=a2a_recv.at[k, p],
                 device_id=device(d), device_id_type=MESH,
             ).start()
             return carry
 
         lax.fori_loop(1, count, push, 0)
-        pltpu.make_async_copy(dst, dst, a2a_recv.at[k]).wait()
+
+    def arrived(k, p, dst):
+        pltpu.make_async_copy(dst.at[p], dst.at[p], a2a_recv.at[k, p]).wait()
 
     on_circ = lambda d: (i, d)
     on_ax = lambda d: (d, j)
 
-    exchange(0, s1, r1, NJ, j, on_circ)
+    for p in range(3):
+        near, far = pulled(load_v[p], stress, p)
+        mixed = dot3_t(*basis_t, near - dot3(far, *slope))
+        for cl in range(4):
+            s1[p, :, cl, :] = mixed[32 * cl : 32 * cl + 32]
+        start(0, p, s1, r1, NJ, j, on_circ)
+
     table_copies[0].wait()
-    lines = [jnp.concatenate([r1[:, 4 * p + cl, :] for cl in range(4)], axis=0) for p in range(3)]
-    blocks = cycle_forward(lines, table_v[0, 0], table_v[0, 1])
     for p in range(3):
-        for it in range(4):
+        arrived(0, p, r1)
+        line = jnp.concatenate([r1[p, :, cl, :] for cl in range(4)], axis=0)
+        for it, four in enumerate(cycle_forward(line, table_v[0, 0], table_v[0, 1])):
             for i4 in range(4):
-                s2[4 * it + i4, p] = blocks[p][it][i4]
-
-    exchange(1, s2, r2, NX, i, on_ax)
+                s2[p, 4 * it + i4] = four[i4]
+        start(1, p, s2, r2, NX, i, on_ax)
+
     table_copies[1].wait()
     table_copies[2].wait()
-    lines = [r2[:, p].reshape(128, 128) for p in range(3)]
-    solved = axial_solve(lines, denom, (table_v[1, 0], table_v[1, 1]), (table_v[2, 0], table_v[2, 1]))
     for p in range(3):
-        s3[:, p] = solved[p].reshape(NX, 8, 128)
-
-    exchange(2, s3, r3, NX, i, on_ax)
+        arrived(1, p, r2)
+        line = r2[p].reshape(128, 128)
+        solved = axial_solve(line, denom, (table_v[1, 0], table_v[1, 1]), (table_v[2, 0], table_v[2, 1]))
+        s3[p] = solved.reshape(NX, 8, 128)
+        start(2, p, s3, r3, NX, i, on_ax)
+
     table_copies[3].wait()
-    blocks = [[[r3[4 * it + i4, p] for i4 in range(4)] for it in range(4)] for p in range(3)]
-    y = cycle_inverse(blocks, table_v[3, 0], table_v[3, 1])
     for p in range(3):
+        arrived(2, p, r3)
+        blocks = [[r3[p, 4 * it + i4] for i4 in range(4)] for it in range(4)]
+        y = cycle_inverse(blocks, table_v[3, 0], table_v[3, 1])
         for c4 in range(4):
-            s4[:, 4 * p + c4, :] = y[32 * p : 32 * p + 32, 128 * c4 : 128 * (c4 + 1)]
-
-    exchange(3, s4, r4, NJ, j, on_circ)
-    lines = [jnp.concatenate([r4[:, 4 * p + c4, :] for c4 in range(4)], axis=0) for p in range(3)]
-    out_v[...] = radial_inverse(lines, *basis_t)
+            s4[p, :, c4, :] = y[:, 128 * c4 : 128 * (c4 + 1)]
+        start(3, p, s4, r4, NJ, j, on_circ)
+
+    for p in range(3):
+        arrived(3, p, r4)
+        line = jnp.concatenate([r4[p, :, c4, :] for c4 in range(4)], axis=0)
+        out_v[128 * p : 128 * (p + 1), :] = dot3(line.T, *basis_t)
 
     for copy in copies:
         copy.wait_send()
     for k, (ref, count) in enumerate(((s1, NJ), (s2, NX), (s3, NX), (s4, NJ))):
-        sent = ref.at[pl.ds(0, count - 1)]
+        sent = ref.at[:, pl.ds(0, count - 1)]
         pltpu.make_async_copy(sent, sent, a2a_send.at[k]).wait()
 
 
@@ -401,24 +422,27 @@
                 pltpu.VMEM((4, 2, 512, 512), BF16),
                 pltpu.VMEM((2, 32, 128), F32),
                 pltpu.VMEM((2, 16, 512), F32),
+                pltpu.VMEM((2, 4, 32, 128), F32),
                 pltpu.VMEM((16, 512), F32),
                 pltpu.VMEM((16, 512), F32),
+                pltpu.VMEM((4, 32, 128), F32),
+                pltpu.VMEM((4, 32, 128), F32),
                 pltpu.VMEM((2, 2, 16, 128), F32),
                 pltpu.VMEM((9, 40, 768), F32),
-                pltpu.VMEM((NJ, 12, 128), F32),
-                pltpu.VMEM((NJ, 12, 128), F32),
-                pltpu.VMEM((NX, 3, 8, 128), F32),
-                pltpu.VMEM((NX, 3, 8, 128), F32),
-                pltpu.VMEM((NX, 3, 8, 128), F32),
-                pltpu.VMEM((NX, 3, 8, 128), F32),
-                pltpu.VMEM((NJ, 12, 128), F32),
-                pltpu.VMEM((NJ, 12, 128), F32),
+                pltpu.VMEM((3, NJ, 4, 128), F32),
+                pltpu.VMEM((3, NJ, 4, 128), F32),
+                pltpu.VMEM((3, NX, 8, 128), F32),
+                pltpu.VMEM((3, NX, 8, 128), F32),
+                pltpu.VMEM((3, NX, 8, 128), F32),
+                pltpu.VMEM((3, NX, 8, 128), F32),
+                pltpu.VMEM((3, NJ, 4, 128), F32),
+                pltpu.VMEM((3, NJ, 4, 128), F32),
                 dma((10,)),
                 dma((4,)),
-                dma((12,)),
-                dma((12,)),
+                dma((8,)),
+                dma((8,)),
                 dma((4,)),
-                dma((4,)),
+                dma((4, 3)),
             ],
             compiler_params=pltpu.CompilerParams(
                 collective_id=0, has_side_effects=True, vmem_limit_bytes=60 * 1024 * 1024

time: 61.1 us -> 56.7 us (0.928)
  Pallas kernels: 59.4 us -> 54.9 us
    pallas_call x1, Pallas kernels: 59.4 us -> 54.9 us  [body(): pl.pallas_call(kernel, out_shape=jax.ShapeDtypeStruct((384, 128), F32), i...]
where the time goes in v2:
time: 56.7 us; the launch traced here: 56.5 us
  Pallas kernels  54.9 us (97%)
  local copies, waits for them, and re-layouts  1.62 us (3%)
    pallas_call x1, Pallas kernels, body(): pl.pallas_call(kernel, out_shape=jax.ShapeDtypeStruct((384, 128), F32), i...  54.9 us
    unnamed x1, local copies, waits for them, and re-layouts  1.62 us

profile of v2, /device:TPU:1, one launch (start us, length us, event | category | flops | bytes accessed | tf_op | source)
XLA Modules:
  0.0 56.5 jit_solution(11724267043691100308)
XLA Ops:
  0.0 54.9 %shard_map.109 = f32[384,128]{1,0:T(8,128)} custom-call(f32[3,32,512]{2,1,0:T(8,128)} %displace.1, f32[3,32,512]{2,1,0:T(8,128)} %load.1, f32[9,32,512]{2,1,0:T(8,128)} %history.1, f32[32,512]{1,0:T(8,128)} %stiffen.1, bf16[4,2,512,512]{3,2,1,0:T(8,128)(2,1)} %constant.2.clone.table, f32[32,32]{1,0:T(8,128)} %slope_hbm.1, f32[32,32]{1,0:T(8,128)} %basis_hbm.1, ...), custom_call_target="tpu_custom_call" | custom-call | tf_op jit(solution)/shard_map/pallas_call | solution.py:406
  54.9 1.6 %copy.15 = f32[3,1,16384]{2,1,0:T(1,128)} copy(f32[3,1,16384]{2,1,0:T(1,128)} %bitcast.3) | data formatting | bytes 393216

commit v3 on v2

--- a/solution.py
+++ b/solution.py
@@ -205,7 +205,7 @@
     slope_ref, basis_ref, axial_ref, cycle_ref, modulus, radial,
     dext, hext, sext, load_v, table_v, pad_v, rsend, csend, rtop, rbot, cleft, cright, corner, stress_v,
     s1, r1, s2, r2, s3, r3, s4, r4,
-    in_sem, table_sem, halo_send, halo_recv, a2a_send, a2a_recv,
+    in_sem, table_sem, halo_send, halo_recv, a2a_send, a2a_recv, known,
 ):
     i = lax.axis_index("ax")
     j = lax.axis_index("circ")
@@ -230,19 +230,22 @@
 
     barrier = pltpu.get_barrier_semaphore()
 
-    def greet_circ(s, carry):
-        pl.semaphore_signal(barrier, inc=1, device_id=(i, lax.rem(j + s, NJ)), device_id_type=MESH)
-        return carry
-
-    def greet_ax(s, carry):
-        pl.semaphore_signal(barrier, inc=1, device_id=(lax.rem(i + s, NX), j), device_id_type=MESH)
-        return carry
+    def near_z(side, step):
+        y_lo, z, core = lax.div(j, 16), lax.rem(lax.div(j, 2), 8), lax.rem(j, 2)
+        y_lo = lax.rem(y_lo + side // 2, 2)
+        core = lax.rem(core + side % 2, 2)
+        return y_lo * 16 + lax.rem(z + step, 8) * 2 + core
+
+    def signal(sem, di, dj):
+        pl.semaphore_signal(sem, inc=1, device_id=(di, dj), device_id_type=MESH)
 
     for di in (up_i, down_i):
-        for dj in (left_j, right_j):
-            pl.semaphore_signal(barrier, inc=1, device_id=(di, dj), device_id_type=MESH)
-    lax.fori_loop(1, NX, greet_ax, 0)
-    lax.fori_loop(1, NJ, greet_circ, 0)
+        for dj in (left_j, right_j, j):
+            signal(barrier, di, dj)
+    for side in range(4):
+        for step in (7, 1, 0):
+            if side or step:
+                signal(barrier, i, near_z(side, step))
     for copy in table_copies:
         copy.start()
 
@@ -260,7 +263,7 @@
         for t, value in enumerate(pack_columns(edge, side == 1)):
             csend[side, t] = value
 
-    pl.semaphore_wait(barrier, NJ - 1 + NX - 1 + 4)
+    pl.semaphore_wait(barrier, 17)
 
     copies = []
 
@@ -282,6 +285,19 @@
     send(rsend.at[0, :, 384:512], corner.at[1, 0], (up_i, right_j))
     send(rsend.at[0, :, 0:128], corner.at[1, 1], (up_i, left_j))
 
+    def tell_z(k, step):
+        for way in (step, 8 - step):
+            signal(known.at[k], i, near_z(0, way))
+
+    def tell_ax(k, step):
+        for way in (step, NX - step):
+            signal(known.at[k], lax.rem(i + way, NX), j)
+
+    def hear(k):
+        pl.semaphore_wait(known.at[k], 2)
+
+    tell_z(0, 1)
+    tell_ax(2, 1)
     for copy in own[3:]:
         copy.wait()
     pad_v[...] = jnp.zeros_like(pad_v)
@@ -296,6 +312,10 @@
     picked = jnp.where(lane == row + 32 * i, jnp.broadcast_to(cycle_ref[...], (32, NC)), 0.0)
     denom = axial_ref[...] + jnp.sum(picked, axis=1, keepdims=True) + radial[j]
 
+    hear(0)
+    tell_z(1, 2)
+    hear(2)
+    tell_ax(3, 2)
     for copy in copies:
         copy.wait_recv()
     not_first, not_last = i > 0, i < NX - 1
@@ -356,8 +376,12 @@
         mixed = dot3_t(*basis_t, near - dot3(far, *slope))
         for cl in range(4):
             s1[p, :, cl, :] = mixed[32 * cl : 32 * cl + 32]
+        if p == 0:
+            hear(1)
         start(0, p, s1, r1, NJ, j, on_circ)
 
+    hear(3)
+    tell_ax(4, 4)
     table_copies[0].wait()
     for p in range(3):
         arrived(0, p, r1)
@@ -365,6 +389,8 @@
         for it, four in enumerate(cycle_forward(line, table_v[0, 0], table_v[0, 1])):
             for i4 in range(4):
                 s2[p, 4 * it + i4] = four[i4]
+        if p == 0:
+            hear(4)
         start(1, p, s2, r2, NX, i, on_ax)
 
     table_copies[1].wait()
@@ -405,7 +431,7 @@
         dma = pltpu.SemaphoreType.DMA
         out = pl.pallas_call(
             kernel,
-            out_shape=jax.ShapeDtypeStruct((384, 128), F32),
+            out_shape=pltpu.VMEM((384, 128), F32),
             in_specs=[hbm] * 11,
             out_specs=pl.BlockSpec(memory_space=pltpu.VMEM),
             scratch_shapes=[
@@ -443,6 +469,7 @@
                 dma((8,)),
                 dma((4,)),
                 dma((4, 3)),
+                pltpu.SemaphoreType.REGULAR((5,)),
             ],
             compiler_params=pltpu.CompilerParams(
                 collective_id=0, has_side_effects=True, vmem_limit_bytes=60 * 1024 * 1024

time: 56.7 us -> 53.8 us (0.949)
  Pallas kernels: 54.9 us -> 53 us
  local copies, waits for them, and re-layouts: 1.62 us -> 0.68 us
    pallas_call x1, Pallas kernels: 54.9 us -> 53 us  [body(): pl.pallas_call(kernel, out_shape=pltpu.VMEM((384, 128), F32), in_specs=[h...]
    unnamed x1, local copies, waits for them, and re-layouts: 1.62 us -> 0.68 us
where the time goes in v3:
time: 53.8 us; the launch traced here: 53.7 us
  Pallas kernels  53 us (99%)
  local copies, waits for them, and re-layouts  0.68 us (1%)
    pallas_call x1, Pallas kernels, body(): pl.pallas_call(kernel, out_shape=pltpu.VMEM((384, 128), F32), in_specs=[h...  53 us

profile of v3, /device:TPU:1, one launch (start us, length us, event | category | flops | bytes accessed | tf_op | source)
XLA Modules:
  0.0 53.7 jit_solution(6862166634310058922)
XLA Ops:
  0.0 53.0 %shard_map.109 = f32[384,128]{1,0:T(8,128)S(1)} custom-call(f32[3,32,512]{2,1,0:T(8,128)} %displace.1, f32[3,32,512]{2,1,0:T(8,128)} %load.1, f32[9,32,512]{2,1,0:T(8,128)} %history.1, f32[32,512]{1,0:T(8,128)} %stiffen.1, bf16[4,2,512,512]{3,2,1,0:T(8,128)(2,1)} %constant.2.clone.table, f32[32,32]{1,0:T(8,128)} %slope_hbm.1, f32[32,32]{1,0:T(8,128)} %basis_hbm.1, ...), custom_call_target="tpu_custom_call" | custom-call | tf_op jit(solution)/shard_map/pallas_call | solution.py:432
  53.0 0.7 %copy.15 = f32[3,1,16384]{2,1,0:T(1,128)} copy(f32[3,1,16384]{2,1,0:T(1,128)S(1)} %bitcast.3) | data formatting | bytes 393216

commit v4 on v3

--- a/solution.py
+++ b/solution.py
@@ -352,24 +352,27 @@
     def stress(m):
         return stress_v[m, 0:32, :], stress_v[m, 1:33, :], stress_v[m, 2:34, :]
 
-    def start(k, p, src, dst, count, me, device):
-        pltpu.make_async_copy(src.at[p, me], dst.at[p, me], a2a_recv.at[k, p]).start()
-
-        def push(s, carry):
-            d = lax.rem(me + s, count)
+    y_hi, x = lax.div(i, 4), lax.rem(i, 4)
+    y_lo, z, core = lax.div(j, 16), lax.rem(lax.div(j, 2), 8), lax.rem(j, 2)
+    at_y = [16 * lax.rem(y_lo + dy, 2) for dy in range(2)]
+    at_z = [2 * lax.rem(z + dz, 8) for dz in range(8)]
+    at_core = [lax.rem(core + dc, 2) for dc in range(2)]
+    at_y_hi = [4 * lax.rem(y_hi + dy, 4) for dy in range(4)]
+    at_x = [lax.rem(x + dx, 4) for dx in range(4)]
+    far_circ = [at_y[dy] + at_z[dz] + at_core[dc] for dz in (4, 3, 5, 2, 6, 1, 7, 0) for dy in (1, 0) for dc in (1, 0)][:-1]
+    far_ax = [at_y_hi[dy] + at_x[dx] for dy in (2, 1, 3, 0) for dx in (2, 1, 3, 0)][:-1]
+
+    def start(k, p, src, dst, on_circ):
+        me = j if on_circ else i
+        for d in far_circ if on_circ else far_ax:
             pltpu.make_async_remote_copy(
                 src_ref=src.at[p, d], dst_ref=dst.at[p, me], send_sem=a2a_send.at[k], recv_sem=a2a_recv.at[k, p],
-                device_id=device(d), device_id_type=MESH,
+                device_id=(i, d) if on_circ else (d, j), device_id_type=MESH,
             ).start()
-            return carry
-
-        lax.fori_loop(1, count, push, 0)
+        pltpu.make_async_copy(src.at[p, me], dst.at[p, me], a2a_recv.at[k, p]).start()
 
     def arrived(k, p, dst):
         pltpu.make_async_copy(dst.at[p], dst.at[p], a2a_recv.at[k, p]).wait()
-
-    on_circ = lambda d: (i, d)
-    on_ax = lambda d: (d, j)
 
     for p in range(3):
         near, far = pulled(load_v[p], stress, p)
@@ -378,7 +381,7 @@
             s1[p, :, cl, :] = mixed[32 * cl : 32 * cl + 32]
         if p == 0:
             hear(1)
-        start(0, p, s1, r1, NJ, j, on_circ)
+        start(0, p, s1, r1, True)
 
     hear(3)
     tell_ax(4, 4)
@@ -391,7 +394,7 @@
                 s2[p, 4 * it + i4] = four[i4]
         if p == 0:
             hear(4)
-        start(1, p, s2, r2, NX, i, on_ax)
+        start(1, p, s2, r2, False)
 
     table_copies[1].wait()
     table_copies[2].wait()
@@ -400,7 +403,7 @@
         line = r2[p].reshape(128, 128)
         solved = axial_solve(line, denom, (table_v[1, 0], table_v[1, 1]), (table_v[2, 0], table_v[2, 1]))
         s3[p] = solved.reshape(NX, 8, 128)
-        start(2, p, s3, r3, NX, i, on_ax)
+        start(2, p, s3, r3, False)
 
     table_copies[3].wait()
     for p in range(3):
@@ -409,7 +412,7 @@
         y = cycle_inverse(blocks, table_v[3, 0], table_v[3, 1])
         for c4 in range(4):
             s4[p, :, c4, :] = y[:, 128 * c4 : 128 * (c4 + 1)]
-        start(3, p, s4, r4, NJ, j, on_circ)
+        start(3, p, s4, r4, True)
 
     for p in range(3):
         arrived(3, p, r4)

time: 53.8 us -> 51.7 us (0.961)
  Pallas kernels: 53 us -> 50.9 us
    pallas_call x1, Pallas kernels: 53 us -> 50.9 us  [body(): pl.pallas_call(kernel, out_shape=pltpu.VMEM((384, 128), F32), in_specs=[h...]
where the time goes in v4:
time: 51.7 us; the launch traced here: 51.6 us
  Pallas kernels  50.9 us (98%)
  local copies, waits for them, and re-layouts  0.68 us (1%)
    pallas_call x1, Pallas kernels, body(): pl.pallas_call(kernel, out_shape=pltpu.VMEM((384, 128), F32), in_specs=[h...  50.9 us

profile of v4, /device:TPU:1, one launch (start us, length us, event | category | flops | bytes accessed | tf_op | source)
XLA Modules:
  0.0 51.6 jit_solution(7733995314408923305)
XLA Ops:
  0.0 50.9 %shard_map.109 = f32[384,128]{1,0:T(8,128)S(1)} custom-call(f32[3,32,512]{2,1,0:T(8,128)} %displace.1, f32[3,32,512]{2,1,0:T(8,128)} %load.1, f32[9,32,512]{2,1,0:T(8,128)} %history.1, f32[32,512]{1,0:T(8,128)} %stiffen.1, bf16[4,2,512,512]{3,2,1,0:T(8,128)(2,1)} %constant.2.clone.table, f32[32,32]{1,0:T(8,128)} %slope_hbm.1, f32[32,32]{1,0:T(8,128)} %basis_hbm.1, ...), custom_call_target="tpu_custom_call" | custom-call | tf_op jit(solution)/shard_map/pallas_call | solution.py:435
  50.9 0.7 %copy.15 = f32[3,1,16384]{2,1,0:T(1,128)} copy(f32[3,1,16384]{2,1,0:T(1,128)S(1)} %bitcast.3) | data formatting | bytes 393216

commit v5 on v4

--- a/solution.py
+++ b/solution.py
@@ -159,9 +159,9 @@
     return [swap_groups(rows(t, 8)) for t in tiles(y)]
 
 
-def axial_solve(x, denom, forward, inverse):
+def axial_solve(x, weight, forward, inverse):
     modes = dot3(jnp.concatenate(rows(x.T, 32), axis=1), *forward)
-    y = dot3(modes / denom, *inverse)
+    y = dot3(modes * weight, *inverse)
     return jnp.concatenate(tiles(y), axis=0).T
 
 
@@ -310,7 +310,7 @@
     lane = lax.broadcasted_iota(jnp.int32, (32, NC), 1)
     row = lax.broadcasted_iota(jnp.int32, (32, NC), 0)
     picked = jnp.where(lane == row + 32 * i, jnp.broadcast_to(cycle_ref[...], (32, NC)), 0.0)
-    denom = axial_ref[...] + jnp.sum(picked, axis=1, keepdims=True) + radial[j]
+    weight = 1.0 / (axial_ref[...] + jnp.sum(picked, axis=1, keepdims=True) + radial[j])
 
     hear(0)
     tell_z(1, 2)
@@ -339,15 +339,15 @@
     grads = gradients(windows, slope_t)
     inside = lax.broadcasted_iota(jnp.int32, (40, 128), 0)
     keep = ((inside > 0) | not_first) & ((inside < 33) | not_last)
-    for t in range(6):
-        cols = slice(128 * t, 128 * (t + 1))
-        piece = [g[:, cols] for g in grads]
-        factor = 1.0 + sext[7:47, cols]
-        for m in range(9):
-            total = modulus[m, 0] * piece[0]
+    factor = [1.0 + sext[7:47, 128 * t : 128 * (t + 1)] for t in range(6)]
+
+    def couple(m):
+        for t in range(6):
+            cols = slice(128 * t, 128 * (t + 1))
+            total = modulus[m, 0] * grads[0][:, cols]
             for n in range(1, 9):
-                total = total + modulus[m, n] * piece[n]
-            stress_v[m, :, cols] = jnp.where(keep, factor * total + hext[m, 7:47, cols], 0.0)
+                total = total + modulus[m, n] * grads[n][:, cols]
+            stress_v[m, :, cols] = jnp.where(keep, factor[t] * total + hext[m, 7:47, cols], 0.0)
 
     def stress(m):
         return stress_v[m, 0:32, :], stress_v[m, 1:33, :], stress_v[m, 2:34, :]
@@ -375,6 +375,8 @@
         pltpu.make_async_copy(dst.at[p], dst.at[p], a2a_recv.at[k, p]).wait()
 
     for p in range(3):
+        for m in (p, 3 + p, 6 + p):
+            couple(m)
         near, far = pulled(load_v[p], stress, p)
         mixed = dot3_t(*basis_t, near - dot3(far, *slope))
         for cl in range(4):
@@ -401,7 +403,7 @@
     for p in range(3):
         arrived(1, p, r2)
         line = r2[p].reshape(128, 128)
-        solved = axial_solve(line, denom, (table_v[1, 0], table_v[1, 1]), (table_v[2, 0], table_v[2, 1]))
+        solved = axial_solve(line, weight, (table_v[1, 0], table_v[1, 1]), (table_v[2, 0], table_v[2, 1]))
         s3[p] = solved.reshape(NX, 8, 128)
         start(2, p, s3, r3, False)
 

time: 51.7 us -> 51.2 us (level)
  no operation moved by 1% of the time
where the time goes in v5:
time: 51.2 us; the launch traced here: 51.1 us
  Pallas kernels  50.4 us (98%)
  local copies, waits for them, and re-layouts  0.68 us (1%)
    pallas_call x1, Pallas kernels, body(): pl.pallas_call(kernel, out_shape=pltpu.VMEM((384, 128), F32), in_specs=[h...  50.4 us

profile of v5, /device:TPU:1, one launch (start us, length us, event | category | flops | bytes accessed | tf_op | source)
XLA Modules:
  0.0 51.1 jit_solution(6135217171403758214)
XLA Ops:
  0.0 50.4 %shard_map.109 = f32[384,128]{1,0:T(8,128)S(1)} custom-call(f32[3,32,512]{2,1,0:T(8,128)} %displace.1, f32[3,32,512]{2,1,0:T(8,128)} %load.1, f32[9,32,512]{2,1,0:T(8,128)} %history.1, f32[32,512]{1,0:T(8,128)} %stiffen.1, bf16[4,2,512,512]{3,2,1,0:T(8,128)(2,1)} %constant.2.clone.table, f32[32,32]{1,0:T(8,128)} %slope_hbm.1, f32[32,32]{1,0:T(8,128)} %basis_hbm.1, ...), custom_call_target="tpu_custom_call" | custom-call | tf_op jit(solution)/shard_map/pallas_call | solution.py:437
  50.4 0.7 %copy.15 = f32[3,1,16384]{2,1,0:T(1,128)} copy(f32[3,1,16384]{2,1,0:T(1,128)S(1)} %bitcast.3) | data formatting | bytes 393216

commit v6 on v5

--- a/solution.py
+++ b/solution.py
@@ -276,14 +276,14 @@
         copy.start()
         copies.append(copy)
 
+    send(rsend.at[1, :, 384:512], corner.at[0, 0], (down_i, right_j))
+    send(rsend.at[1, :, 0:128], corner.at[0, 1], (down_i, left_j))
+    send(rsend.at[0, :, 384:512], corner.at[1, 0], (up_i, right_j))
+    send(rsend.at[0, :, 0:128], corner.at[1, 1], (up_i, left_j))
     send(rsend.at[1], rtop, (down_i, j))
     send(rsend.at[0], rbot, (up_i, j))
     send(csend.at[1], cleft, (i, right_j))
     send(csend.at[0], cright, (i, left_j))
-    send(rsend.at[1, :, 384:512], corner.at[0, 0], (down_i, right_j))
-    send(rsend.at[1, :, 0:128], corner.at[0, 1], (down_i, left_j))
-    send(rsend.at[0, :, 384:512], corner.at[1, 0], (up_i, right_j))
-    send(rsend.at[0, :, 0:128], corner.at[1, 1], (up_i, left_j))
 
     def tell_z(k, step):
         for way in (step, 8 - step):
@@ -316,7 +316,7 @@
     tell_z(1, 2)
     hear(2)
     tell_ax(3, 2)
-    for copy in copies:
+    for copy in copies[6:]:
         copy.wait_recv()
     not_first, not_last = i > 0, i < NX - 1
     for ref, cols, left in ((cleft, slice(0, 128), True), (cright, slice(640, 768), False)):
@@ -326,6 +326,8 @@
         for n in range(9):
             hext[n, 8:40, cols] = fields[3 + n]
         sext[8:40, cols] = fields[12]
+    for copy in copies[:6]:
+        copy.wait_recv()
     for side, (ref, d0, h0, there) in enumerate(((rtop, 6, 7, not_first), (rbot, 40, 40, not_last))):
         whole = jnp.concatenate([corner[side, 0], ref[...], corner[side, 1]], axis=1)
         whole = jnp.where(there, whole, 0.0)

time: 51.2 us -> 49.9 us (0.975)
  Pallas kernels: 50.4 us -> 49.1 us
    pallas_call x1, Pallas kernels: 50.4 us -> 49.1 us  [body(): pl.pallas_call(kernel, out_shape=pltpu.VMEM((384, 128), F32), in_specs=[h...]
where the time goes in v6:
time: 49.9 us; the launch traced here: 49.8 us
  Pallas kernels  49.1 us (98%)
  local copies, waits for them, and re-layouts  0.68 us (1%)
    pallas_call x1, Pallas kernels, body(): pl.pallas_call(kernel, out_shape=pltpu.VMEM((384, 128), F32), in_specs=[h...  49.1 us

profile of v6, /device:TPU:1, one launch (start us, length us, event | category | flops | bytes accessed | tf_op | source)
XLA Modules:
  0.0 49.8 jit_solution(14458456679758370290)
XLA Ops:
  0.0 49.1 %shard_map.109 = f32[384,128]{1,0:T(8,128)S(1)} custom-call(f32[3,32,512]{2,1,0:T(8,128)} %displace.1, f32[3,32,512]{2,1,0:T(8,128)} %load.1, f32[9,32,512]{2,1,0:T(8,128)} %history.1, f32[32,512]{1,0:T(8,128)} %stiffen.1, bf16[4,2,512,512]{3,2,1,0:T(8,128)(2,1)} %constant.2.clone.table, f32[32,32]{1,0:T(8,128)} %slope_hbm.1, f32[32,32]{1,0:T(8,128)} %basis_hbm.1, ...), custom_call_target="tpu_custom_call" | custom-call | tf_op jit(solution)/shard_map/pallas_call | solution.py:439
  49.1 0.7 %copy.15 = f32[3,1,16384]{2,1,0:T(1,128)} copy(f32[3,1,16384]{2,1,0:T(1,128)S(1)} %bitcast.3) | data formatting | bytes 393216

commit v7 on v6

--- a/solution.py
+++ b/solution.py
@@ -246,8 +246,6 @@
         for step in (7, 1, 0):
             if side or step:
                 signal(barrier, i, near_z(side, step))
-    for copy in table_copies:
-        copy.start()
 
     for copy in own[:3]:
         copy.wait()
@@ -284,6 +282,8 @@
     send(rsend.at[0], rbot, (up_i, j))
     send(csend.at[1], cleft, (i, right_j))
     send(csend.at[0], cright, (i, left_j))
+    for copy in table_copies:
+        copy.start()
 
     def tell_z(k, step):
         for way in (step, 8 - step):

time: 49.9 us -> 50 us (level)
  no operation moved by 1% of the time
where the time goes in v7:
time: 50 us; the launch traced here: 49.8 us
  Pallas kernels  49.1 us (98%)
  local copies, waits for them, and re-layouts  0.68 us (1%)
    pallas_call x1, Pallas kernels, body(): pl.pallas_call(kernel, out_shape=pltpu.VMEM((384, 128), F32), in_specs=[h...  49.1 us

profile of v7, /device:TPU:1, one launch (start us, length us, event | category | flops | bytes accessed | tf_op | source)
XLA Modules:
  0.0 49.8 jit_solution(7891479554058796543)
XLA Ops:
  0.0 49.1 %shard_map.109 = f32[384,128]{1,0:T(8,128)S(1)} custom-call(f32[3,32,512]{2,1,0:T(8,128)} %displace.1, f32[3,32,512]{2,1,0:T(8,128)} %load.1, f32[9,32,512]{2,1,0:T(8,128)} %history.1, f32[32,512]{1,0:T(8,128)} %stiffen.1, bf16[4,2,512,512]{3,2,1,0:T(8,128)(2,1)} %constant.2.clone.table, f32[32,32]{1,0:T(8,128)} %slope_hbm.1, f32[32,32]{1,0:T(8,128)} %basis_hbm.1, ...), custom_call_target="tpu_custom_call" | custom-call | tf_op jit(solution)/shard_map/pallas_call | solution.py:439
  49.2 0.7 %copy.15 = f32[3,1,16384]{2,1,0:T(1,128)} copy(f32[3,1,16384]{2,1,0:T(1,128)S(1)} %bitcast.3) | data formatting | bytes 393216
